TPU v7x, 32 devices: a whole 2x2x4 slice. The times are simulated.
32 devices in a mesh: slab: 16 (over z, y, core), tile: 2 (over x).
Axes of the slice: x: 2, y: 2, z: 4, core: 2. Of those that a mesh axis runs over, the one named last changes fastest.
Arguments:
- positions: float32 [64, 3, 128], P(('slab', 'tile')), may hold values from 0 to 150
- weights: float32 [64, 128], P(('slab', 'tile')), may hold values from -6 to 6
- counts: int32 [64], P(('slab', 'tile')), may hold values from 64 to 128
- pairs: int32 [32, 8, 2], P(('slab', 'tile')), may hold values from 0 to 7, as said below
- pair_count: int32 [32], P(('slab', 'tile')), may hold values from 1 to 8
Outputs:
- harmonics: float32 [64, 360, 128], P(('slab', 'tile'))
- zeta: float32 [64, 6, 100], P(('slab', 'tile'))
Inputs may be any that keep to these rules, and one draw needn't show every extreme that they name: pairs[d, p, 0] is below 2. pairs[d, p, 1] = h * 2 * 2 + t2 * 2 + k2 names block k2 of tile t2 in the device's slab (h = 0) or in the slab below it (h = 1, never on the first slab); with h = 0 the named block is never earlier in the slab's order of blocks than the local one. Among the first pair_count entries of all devices, each unordered pair of blocks appears at most once; a block paired with itself is allowed.
All inputs are finite; a program needn't handle non-finite values.
Results may differ from a plain program's by a relative error of at most 0.0003.
Values sent between devices are 32-bit elements; how exact they have to be, the bound alone decides.
No kernel may reach another device: no remote copies, remote signals or barrier semaphores. Data moves between devices by JAX's collectives and lax.ppermute only.
A program may use at most 64 MiB of HBM per device.

v0:
```python
import math

import jax
import jax.numpy as jnp
import numpy as np
from jax import lax
from jax.sharding import PartitionSpec as P

PTS = 128
NBIN = 10
NHARM = 36


HIGH = lax.Precision.HIGHEST
reach = 150.0


def passed_along(x, axis, by):
    size = lax.axis_size(axis)
    pairs = [(i, i + by) for i in range(size) if 0 <= i + by < size]
    return lax.ppermute(x, axis, pairs)


def solid_harmonics(unit_x, unit_y, unit_z):
    unity = jnp.ones_like(unit_z)
    cosine_parts = [unity]
    sine_parts = [jnp.zeros_like(unit_z)]
    for azimuth in range(1, 6):
        cosine_prev = cosine_parts[-1]
        sine_prev = sine_parts[-1]
        cosine_parts.append(cosine_prev * unit_x - sine_prev * unit_y)
        sine_parts.append(sine_prev * unit_x + cosine_prev * unit_y)
    legendre = {}
    for azimuth in range(6):
        diagonal = float(math.prod(range(2 * azimuth - 1, 0, -2)))
        legendre[azimuth, azimuth] = diagonal * unity
        if azimuth + 1 <= 5:
            legendre[azimuth + 1, azimuth] = (2 * azimuth + 1) * diagonal * unit_z
        for degree in range(azimuth + 2, 6):
            legendre[degree, azimuth] = (
                (2 * degree - 1) * unit_z * legendre[degree - 1, azimuth]
                - (degree + azimuth - 1) * legendre[degree - 2, azimuth]
            ) / (degree - azimuth)
    result = []
    for degree in range(6):
        for signed in range(-degree, degree + 1):
            azimuth = abs(signed)
            factor = math.sqrt(
                (2 * degree + 1)
                / (4 * math.pi)
                * math.factorial(degree - azimuth)
                / math.factorial(degree + azimuth)
            )
            if azimuth > 0:
                factor = factor * math.sqrt(2.0)
            trig = sine_parts[azimuth] if signed < 0 else cosine_parts[azimuth]
            result.append(factor * legendre[degree, azimuth] * trig)
    return jnp.stack(result)


def parity_table():
    return np.array(
        [(-1.0) ** degree for degree in range(6) for _ in range(2 * degree + 1)], dtype=np.float32
    )


def geometry(first_pos, second_pos):
    offset = second_pos[:, None, :] - first_pos[:, :, None]
    distance = jnp.sqrt(jnp.sum(offset * offset, axis=0))
    inverse = 1.0 / jnp.maximum(distance, 1.0)
    harm = solid_harmonics(offset[0] * inverse, offset[1] * inverse, offset[2] * inverse)
    spacing = reach / (NBIN + 1)
    centres = (jnp.arange(NBIN, dtype=jnp.float32) + 1.0) * spacing
    radial = jnp.maximum(0.0, 1.0 - jnp.abs(distance[None] - centres[:, None, None]) / spacing)
    return (harm, radial)


def pair_terms(first_pos, second_pos, first_live, second_live):
    harm, radial = geometry(first_pos, second_pos)
    forward = jnp.einsum("kij,bij->kbi", harm, radial * second_live[None, None, :], precision=HIGH)
    flipped = jnp.einsum("kij,bij->kbj", harm, radial * first_live[None, :, None], precision=HIGH)
    flipped = flipped * jnp.asarray(parity_table())[:, None, None]
    return (forward.reshape(NHARM * NBIN, -1), flipped.reshape(NHARM * NBIN, -1))


def block_zeta(harm_block, live):
    shaped = harm_block.reshape(harm_block.shape[0], NHARM, NBIN, harm_block.shape[-1])
    levels = []
    for degree in range(6):
        piece = shaped[:, degree * degree : (degree + 1) * (degree + 1)]
        value = (
            jnp.einsum("zkxi,zkyi->zxy", piece * live[:, None, None, :], piece, precision=HIGH)
            / PTS
        )
        levels.append(value.reshape(value.shape[0], NBIN * NBIN))
    return jnp.stack(levels, axis=1)


def add_block(accum, index, term):
    row = lax.dynamic_index_in_dim(accum, index, 0, keepdims=False)
    return lax.dynamic_update_index_in_dim(accum, row + term, index, 0)


def shards(positions, weights, counts, pairs, pair_count):
    blocks_here = positions.shape[0]
    points = positions.shape[2]
    slot = jnp.arange(points, dtype=jnp.int32)
    live = weights * (slot[None, :] < counts[:, None]).astype(jnp.float32)
    tiles = lax.axis_size("tile")
    span = tiles * blocks_here
    slab_pos, slab_live = (
        lax.all_gather(positions, "tile", axis=0, tiled=True),
        lax.all_gather(live, "tile", axis=0, tiled=True),
    )
    below_pos, below_live = passed_along((slab_pos, slab_live), "slab", 1)
    set_pos = jnp.concatenate([slab_pos, below_pos], axis=0)
    set_live = jnp.concatenate([slab_live, below_live], axis=0)
    my_tile = lax.axis_index("tile")
    offset_own = my_tile * blocks_here
    accum = jnp.zeros((2 * span, NHARM * NBIN, points), jnp.float32)

    def step(index, accum):
        first_idx = (offset_own + pairs[0, index, 0]).astype(jnp.int32)
        second_idx = pairs[0, index, 1].astype(jnp.int32)
        first_pos = lax.dynamic_index_in_dim(set_pos, first_idx, 0, keepdims=False)
        second_pos = lax.dynamic_index_in_dim(set_pos, second_idx, 0, keepdims=False)
        first_live = lax.dynamic_index_in_dim(set_live, first_idx, 0, keepdims=False)
        second_live = lax.dynamic_index_in_dim(set_live, second_idx, 0, keepdims=False)
        forward, flipped = pair_terms(first_pos, second_pos, first_live, second_live)
        accum = add_block(accum, first_idx, forward)
        other = jnp.where(first_idx == second_idx, 0.0, 1.0).astype(jnp.float32)
        return add_block(accum, second_idx, other * flipped)

    accum = lax.fori_loop(0, pair_count[0], step, accum)
    returned = passed_along(accum[span:], "slab", -1)
    mine_sum = accum[:span] + returned
    total = lax.psum_scatter(mine_sum, "tile", scatter_dimension=0, tiled=True)
    return (total, block_zeta(total, live))


def solution(mesh):
    return jax.shard_map(
        shards,
        mesh=mesh,
        in_specs=(
            P(("slab", "tile"), None, None),
            P(("slab", "tile"), None),
            P(("slab", "tile")),
            P(("slab", "tile"), None, None),
            P(("slab", "tile")),
        ),
        out_specs=(P(("slab", "tile"), None, None), P(("slab", "tile"), None, None)),
        check_vma=False,
    )
```

profile of v0, /device:TPU:1, one launch (start us, length us, event | category | flops | bytes accessed | tf_op | source)
XLA Modules:
  0.0 309.3 jit_solution(3987315245459001118)
XLA Ops:
  8.0 3.6 %all-gather = f32[2,2,128]{2,1,0:T(2,128)S(1)} all-gather(f32[1,2,128]{2,1,0:T(2,128)S(1)} %fusion.49), channel_id=1, replica_groups=mesh['slab'=16,'tile'=2] {'tile'}, dimensions={0}, use_global_device_ids=true | all-gather | bytes 3072 | tf_op jit(solution)/shard_map/all_gather | solution.py:113
  11.6 5.1 %collective-permute-start.1 = (f32[4,128]{1,0:T(4,128)S(1)}, f32[4,128]{1,0:T(4,128)S(1)}, u32[]{:S(2)}, u32[]{:S(2)}) collective-permute-start(f32[4,128]{1,0:T(4,128)S(1)} %bitcast.81), channel_id=1, source_target_pairs={{0,2},{2,4},{4,6},{6,8},{8,10},{10,12},{12,14},{14,16},{16,18},{18... | collective-permute-start | bytes 6152 | tf_op jit(solution)/shard_map/ppermute | solution.py:21
  17.4 3.2 %all_gather.6 = f32[4,3,128]{2,1,0:T(4,128)S(1)} all-gather(f32[2,3,128]{2,1,0:T(4,128)S(1)} %copy.69), channel_id=1, replica_groups=mesh['slab'=16,'tile'=2] {'tile'}, dimensions={0}, use_global_device_ids=true | all-gather | bytes 9216 | tf_op jit(solution)/shard_map/all_gather | solution.py:112
  20.6 3.1 collective-permute-start
  25.7 244.2 %while.13 = (s32[]{:T(128)}, f32[8,360,128]{2,1,0:T(8,128)}, s32[]{:T(128)}, s32[1,8,2]{1,2,0:T(2,128)}, s32[]{:T(128)}, /*index=5*/f32[8,3,128]{2,1,0:T(4,128)S...) while((s32[]{:T(128)}, f32[8,360,128]{2,1,0:T(8,128)}, ...), condition=%wide.region_2.3_spmd.clone, body=%wide.region_0.2_spmd.sunk.clone.sunk | while | flops 151572512 | bytes 24671412 | solution.py:134
  32.0 2.2 copy.128
  35.0 6.0 %fusion.67 = f32[36,10,128]{0,1,2:T(8,128)S(1)} fusion(f32[36,128,128]{1,0,2:T(8,128)} %copy.128, f32[36]{0:T(128)S(1)} %copy-done.1, f32[128]{0:T(128)S(1)} %get-tuple-element.250, f32[]{:T(128)S(6)} %select_n.51, f32[10]{0:T(128)S(1)} %add_multiply_fusion.3, f32[128,128]{0,1:T(8,128)S(1)} %copy.125), kind=kOutput, calls=%fused_computation.5.clone.1 | convolution fusion | flops 71854080 | bytes 2609852 | tf_op jit(solution)/shard_map/while/body/kij,bij->kbj/dot_general | solution.py:81
  42.2 1.6 mul.2976
  45.9 6.4 %fusion.66 = f32[36,10,128]{0,1,2:T(8,128)S(1)} fusion(f32[10,128,128]{2,0,1:T(8,128)} %copy.126, f32[36,128,128]{2,1,0:T(8,128)S(1)} %constant_dynamic-update-slice_fusion.113), kind=kOutput, calls=%fused_computation.2.clone.1 | convolution fusion | flops 70778880 | bytes 3198976 | tf_op jit(solution)/shard_map/while/body/kij,bij->kbi/dot_general | solution.py:80
  52.8 1.6 add_dynamic-update-slice_fusion.4
  62.4 2.2 copy.128
  65.5 6.0 %fusion.67 = f32[36,10,128]{0,1,2:T(8,128)S(1)} fusion(f32[36,128,128]{1,0,2:T(8,128)} %copy.128, f32[36]{0:T(128)S(1)} %copy-done.1, f32[128]{0:T(128)S(1)} %get-tuple-element.250, f32[]{:T(128)S(6)} %select_n.51, f32[10]{0:T(128)S(1)} %add_multiply_fusion.3, f32[128,128]{0,1:T(8,128)S(1)} %copy.125), kind=kOutput, calls=%fused_computation.5.clone.1 | convolution fusion | flops 71854080 | bytes 2609852 | tf_op jit(solution)/shard_map/while/body/kij,bij->kbj/dot_general | solution.py:81
  72.6 1.6 mul.2976
  76.3 6.4 %fusion.66 = f32[36,10,128]{0,1,2:T(8,128)S(1)} fusion(f32[10,128,128]{2,0,1:T(8,128)} %copy.126, f32[36,128,128]{2,1,0:T(8,128)S(1)} %constant_dynamic-update-slice_fusion.113), kind=kOutput, calls=%fused_computation.2.clone.1 | convolution fusion | flops 70778880 | bytes 3198976 | tf_op jit(solution)/shard_map/while/body/kij,bij->kbi/dot_general | solution.py:80
  83.3 1.6 add_dynamic-update-slice_fusion.4
  92.9 2.2 copy.128
  95.9 6.0 %fusion.67 = f32[36,10,128]{0,1,2:T(8,128)S(1)} fusion(f32[36,128,128]{1,0,2:T(8,128)} %copy.128, f32[36]{0:T(128)S(1)} %copy-done.1, f32[128]{0:T(128)S(1)} %get-tuple-element.250, f32[]{:T(128)S(6)} %select_n.51, f32[10]{0:T(128)S(1)} %add_multiply_fusion.3, f32[128,128]{0,1:T(8,128)S(1)} %copy.125), kind=kOutput, calls=%fused_computation.5.clone.1 | convolution fusion | flops 71854080 | bytes 2609852 | tf_op jit(solution)/shard_map/while/body/kij,bij->kbj/dot_general | solution.py:81
  103.1 1.6 mul.2976
  106.8 6.4 %fusion.66 = f32[36,10,128]{0,1,2:T(8,128)S(1)} fusion(f32[10,128,128]{2,0,1:T(8,128)} %copy.126, f32[36,128,128]{2,1,0:T(8,128)S(1)} %constant_dynamic-update-slice_fusion.113), kind=kOutput, calls=%fused_computation.2.clone.1 | convolution fusion | flops 70778880 | bytes 3198976 | tf_op jit(solution)/shard_map/while/body/kij,bij->kbi/dot_general | solution.py:80
  113.7 1.6 add_dynamic-update-slice_fusion.4
  123.3 2.2 copy.128
  126.3 6.0 %fusion.67 = f32[36,10,128]{0,1,2:T(8,128)S(1)} fusion(f32[36,128,128]{1,0,2:T(8,128)} %copy.128, f32[36]{0:T(128)S(1)} %copy-done.1, f32[128]{0:T(128)S(1)} %get-tuple-element.250, f32[]{:T(128)S(6)} %select_n.51, f32[10]{0:T(128)S(1)} %add_multiply_fusion.3, f32[128,128]{0,1:T(8,128)S(1)} %copy.125), kind=kOutput, calls=%fused_computation.5.clone.1 | convolution fusion | flops 71854080 | bytes 2609852 | tf_op jit(solution)/shard_map/while/body/kij,bij->kbj/dot_general | solution.py:81
  133.5 1.6 mul.2976
  137.2 6.4 %fusion.66 = f32[36,10,128]{0,1,2:T(8,128)S(1)} fusion(f32[10,128,128]{2,0,1:T(8,128)} %copy.126, f32[36,128,128]{2,1,0:T(8,128)S(1)} %constant_dynamic-update-slice_fusion.113), kind=kOutput, calls=%fused_computation.2.clone.1 | convolution fusion | flops 70778880 | bytes 3198976 | tf_op jit(solution)/shard_map/while/body/kij,bij->kbi/dot_general | solution.py:80
  144.2 1.6 add_dynamic-update-slice_fusion.4
  153.8 2.2 copy.128
  156.8 6.0 %fusion.67 = f32[36,10,128]{0,1,2:T(8,128)S(1)} fusion(f32[36,128,128]{1,0,2:T(8,128)} %copy.128, f32[36]{0:T(128)S(1)} %copy-done.1, f32[128]{0:T(128)S(1)} %get-tuple-element.250, f32[]{:T(128)S(6)} %select_n.51, f32[10]{0:T(128)S(1)} %add_multiply_fusion.3, f32[128,128]{0,1:T(8,128)S(1)} %copy.125), kind=kOutput, calls=%fused_computation.5.clone.1 | convolution fusion | flops 71854080 | bytes 2609852 | tf_op jit(solution)/shard_map/while/body/kij,bij->kbj/dot_general | solution.py:81
  164.0 1.6 mul.2976
  167.7 6.4 %fusion.66 = f32[36,10,128]{0,1,2:T(8,128)S(1)} fusion(f32[10,128,128]{2,0,1:T(8,128)} %copy.126, f32[36,128,128]{2,1,0:T(8,128)S(1)} %constant_dynamic-update-slice_fusion.113), kind=kOutput, calls=%fused_computation.2.clone.1 | convolution fusion | flops 70778880 | bytes 3198976 | tf_op jit(solution)/shard_map/while/body/kij,bij->kbi/dot_general | solution.py:80
  184.2 2.2 copy.128
  187.2 6.0 %fusion.67 = f32[36,10,128]{0,1,2:T(8,128)S(1)} fusion(f32[36,128,128]{1,0,2:T(8,128)} %copy.128, f32[36]{0:T(128)S(1)} %copy-done.1, f32[128]{0:T(128)S(1)} %get-tuple-element.250, f32[]{:T(128)S(6)} %select_n.51, f32[10]{0:T(128)S(1)} %add_multiply_fusion.3, f32[128,128]{0,1:T(8,128)S(1)} %copy.125), kind=kOutput, calls=%fused_computation.5.clone.1 | convolution fusion | flops 71854080 | bytes 2609852 | tf_op jit(solution)/shard_map/while/body/kij,bij->kbj/dot_general | solution.py:81
  194.4 1.6 mul.2976
  198.1 6.4 %fusion.66 = f32[36,10,128]{0,1,2:T(8,128)S(1)} fusion(f32[10,128,128]{2,0,1:T(8,128)} %copy.126, f32[36,128,128]{2,1,0:T(8,128)S(1)} %constant_dynamic-update-slice_fusion.113), kind=kOutput, calls=%fused_computation.2.clone.1 | convolution fusion | flops 70778880 | bytes 3198976 | tf_op jit(solution)/shard_map/while/body/kij,bij->kbi/dot_general | solution.py:80
  205.1 1.6 add_dynamic-update-slice_fusion.4
  214.7 2.2 copy.128
  217.7 6.0 %fusion.67 = f32[36,10,128]{0,1,2:T(8,128)S(1)} fusion(f32[36,128,128]{1,0,2:T(8,128)} %copy.128, f32[36]{0:T(128)S(1)} %copy-done.1, f32[128]{0:T(128)S(1)} %get-tuple-element.250, f32[]{:T(128)S(6)} %select_n.51, f32[10]{0:T(128)S(1)} %add_multiply_fusion.3, f32[128,128]{0,1:T(8,128)S(1)} %copy.125), kind=kOutput, calls=%fused_computation.5.clone.1 | convolution fusion | flops 71854080 | bytes 2609852 | tf_op jit(solution)/shard_map/while/body/kij,bij->kbj/dot_general | solution.py:81
  224.9 1.6 mul.2976
  228.6 6.4 %fusion.66 = f32[36,10,128]{0,1,2:T(8,128)S(1)} fusion(f32[10,128,128]{2,0,1:T(8,128)} %copy.126, f32[36,128,128]{2,1,0:T(8,128)S(1)} %constant_dynamic-update-slice_fusion.113), kind=kOutput, calls=%fused_computation.2.clone.1 | convolution fusion | flops 70778880 | bytes 3198976 | tf_op jit(solution)/shard_map/while/body/kij,bij->kbi/dot_general | solution.py:80
  235.5 1.6 add_dynamic-update-slice_fusion.4
  245.1 2.2 copy.128
  248.1 6.0 %fusion.67 = f32[36,10,128]{0,1,2:T(8,128)S(1)} fusion(f32[36,128,128]{1,0,2:T(8,128)} %copy.128, f32[36]{0:T(128)S(1)} %copy-done.1, f32[128]{0:T(128)S(1)} %get-tuple-element.250, f32[]{:T(128)S(6)} %select_n.51, f32[10]{0:T(128)S(1)} %add_multiply_fusion.3, f32[128,128]{0,1:T(8,128)S(1)} %copy.125), kind=kOutput, calls=%fused_computation.5.clone.1 | convolution fusion | flops 71854080 | bytes 2609852 | tf_op jit(solution)/shard_map/while/body/kij,bij->kbj/dot_general | solution.py:81
  255.3 1.6 mul.2976
  259.0 6.4 %fusion.66 = f32[36,10,128]{0,1,2:T(8,128)S(1)} fusion(f32[10,128,128]{2,0,1:T(8,128)} %copy.126, f32[36,128,128]{2,1,0:T(8,128)S(1)} %constant_dynamic-update-slice_fusion.113), kind=kOutput, calls=%fused_computation.2.clone.1 | convolution fusion | flops 70778880 | bytes 3198976 | tf_op jit(solution)/shard_map/while/body/kij,bij->kbi/dot_general | solution.py:80
  266.0 1.6 add_dynamic-update-slice_fusion.4
  271.1 1.9 collective-permute-start.2
  273.0 10.9 %collective-permute-done.2 = f32[4,360,128]{2,1,0:T(8,128)S(1)} collective-permute-done((f32[4,360,128]{2,1,0:T(8,128)S(1)}, f32[4,360,128]{2,1,0:T(8,128)S(1)}, u32[]{:S(2)}, u32[]{:S(2)}) %collective-permute-start.2) | collective-permute-done | bytes 737312 | tf_op jit(solution)/shard_map/ppermute | solution.py:21
  283.9 2.1 slice_add_fusion
  286.0 12.5 %reduce-scatter.2.cloned.1.call-done = f32[2,360,128]{2,1,0:T(8,128)} async-done(((f32[4,360,128]{2,1,0:T(8,128)}), f32[2,360,128]{2,1,0:T(8,128)}) %reduce-scatter.2.cloned.1.call-update) | async-done | bytes 368656 | tf_op jit(solution)/shard_map/reduce_scatter | solution.py:137
  (467 shorter events, 76.9 us)
Async XLA Ops:
  7.2 291.3 %reduce-scatter.2.cloned.1.call-start = ((), (), s32[]{:S(2)}) async-start(), calls=%async_computation.1 | async-start | bytes 1105920 | tf_op jit(solution)/shard_map/reduce_scatter | solution.py:137
  11.6 12.1 %collective-permute-start.1 = (f32[4,128]{1,0:T(4,128)S(1)}, f32[4,128]{1,0:T(4,128)S(1)}, u32[]{:S(2)}, u32[]{:S(2)}) collective-permute-start(f32[4,128]{1,0:T(4,128)S(1)} %bitcast.81), channel_id=1, source_target_pairs={{0,2},{2,4},{4,6},{6,8},{8,10},{10,12},{12,14},{14,16},{16,18},{18... | collective-permute-start | bytes 6152 | tf_op jit(solution)/shard_map/ppermute | solution.py:21
  20.6 3.8 %collective-permute-start = (f32[4,3,128]{2,1,0:T(4,128)S(1)}, f32[4,3,128]{2,1,0:T(4,128)S(1)}, u32[]{:S(2)}, u32[]{:S(2)}) collective-permute-start(f32[4,3,128]{2,1,0:T(4,128)S(1)} %all_gather.6), channel_id=1, source_target_pairs={{0,2},{2,4},{4,6},{6,8},{8,10},{10,12},{12,14},{14,16},{16,18},{18... | collective-permute-start | bytes 18440 | tf_op jit(solution)/shard_map/ppermute | solution.py:21
  32.0 3.0 copy-start.1
  52.3 2.2 copy-start
  62.4 3.0 copy-start.1
  82.7 2.2 copy-start
  92.9 3.0 copy-start.1
  113.2 2.2 copy-start
  123.3 3.0 copy-start.1
  143.6 2.2 copy-start
  153.8 3.0 copy-start.1
  174.1 2.2 copy-start
  184.2 3.0 copy-start.1
  204.5 2.2 copy-start
  214.6 3.0 copy-start.1
  235.0 2.2 copy-start
  245.1 3.0 copy-start.1
  265.4 2.2 copy-start
  269.9 16.1 %copy-start.2 = (f32[2,128]{1,0:T(2,128)S(1)}, f32[2,128]{1,0:T(2,128)}, u32[]{:S(2)}) copy-start(f32[2,128]{1,0:T(2,128)} %param.9) | copy-start | bytes 3076
  269.9 16.1 %copy-start.3 = (s32[2]{0:T(128)S(1)}, s32[2]{0:T(128)}, u32[]{:S(2)}) copy-start(s32[2]{0:T(128)} %param.10) | copy-start | bytes 28
  271.1 12.8 %collective-permute-start.2 = (f32[4,360,128]{2,1,0:T(8,128)S(1)}, f32[4,360,128]{2,1,0:T(8,128)S(1)}, u32[]{:S(2)}, u32[]{:S(2)}) collective-permute-start(f32[4,360,128]{2,1,0:T(8,128)S(1)} %slice.43), channel_id=1, source_target_pairs={{2,0},{4,2},{6,4},{8,6},{10,8},{12,10},{14,12},{16,14},{18,16},{20... | collective-permute-start | bytes 2211848 | tf_op jit(solution)/shard_map/ppermute | solution.py:21
  301.9 0.6 copy-start.4
Sparse Core Ops, SparseCore 0:
  286.1 12.3 reduce-scatter.1
where the time goes:
time: 312 us; the launch traced here: 309 us
  matrix products  101 us (32%)
  local copies, waits for them, and re-layouts  74.9 us (24%)
  other arithmetic  44 us (14%)
  loops' own time  34.6 us (11%)
  waiting for transfers between devices  24.1 us (8%)
  between operations  14.2 us (5%)
  starting transfers between devices  10.1 us (3%)
  blocking collectives  6.82 us (2%)
    dot_general x8, matrix products, pair_terms(): jnp.einsum('kij,bij->kbi', harm, radial * second_live[None, None, :], pre...  51.2 us
    dot_general x8, matrix products, pair_terms(): jnp.einsum('kij,bij->kbj', harm, radial * first_live[None, :, None], prec...  47.8 us
    another operation x1, loops' own time, shards(): accum = lax.fori_loop(0, pair_count[0], step, accum)  34.6 us
    dynamic_update_slice x16, other arithmetic, add_block(): return lax.dynamic_update_index_in_dim(accum, row + term, index, 0)  26 us
    mul x16, local copies, waits for them, and re-layouts, step(): return add_block(accum, second_idx, other * flipped)  22.8 us
    another operation x8, local copies, waits for them, and re-layouts, solid_harmonics(): return jnp.stack(result)  17.7 us
    mul x8, local copies, waits for them, and re-layouts, pair_terms(): radial * second_live[None, None, :]  12.7 us
    reduce_scatter x1, waiting for transfers between devices, shards(): total = lax.psum_scatter(mine_sum, 'tile', scatter_dimension=0, tiled=True)  12.5 us
  transfers between devices with their start and end apart: 4, of which 3 were waited for; matrix products, arithmetic and copies ran while one was open for 0% of the time, Pallas kernels for 0%

commit v1 on v0

v1 whole, which is shorter than its diff:
```python
import math

import jax
import jax.numpy as jnp
from jax import lax
from jax.experimental import pallas as pl
from jax.experimental.pallas import tpu as pltpu
from jax.sharding import PartitionSpec as P

NBIN = 10
DEGREES = 6
NHARM = DEGREES * DEGREES
BPAD = 16
SPACING = 150.0 / (NBIN + 1)
SUB = 8
STEP = 2
HIGH = lax.Precision.HIGHEST


def harmonic_scales():
    out = []
    for l in range(DEGREES):
        for signed in range(-l, l + 1):
            m = abs(signed)
            norm = math.sqrt((2 * l + 1) / (4 * math.pi) * math.factorial(l - m) / math.factorial(l + m))
            if m > 0:
                norm *= math.sqrt(2.0)
            lead = math.prod(range(2 * l - 1, 0, -2)) / math.factorial(l - m)
            out.append(norm * lead)
    return out


def harmonics_of(x, y, z, w):
    s = z * z
    q = {
        (2, 0): s - 1.0 / 3.0,
        (3, 1): s - 0.2,
        (4, 2): s - 1.0 / 7.0,
        (5, 3): s - 1.0 / 9.0,
        (3, 0): z * (s - 0.6),
        (4, 1): z * (s - 3.0 / 7.0),
        (4, 0): s * (s - 6.0 / 7.0) + 3.0 / 35.0,
        (5, 1): s * (s - 2.0 / 3.0) + 1.0 / 21.0,
        (5, 0): z * (s * (s - 10.0 / 9.0) + 5.0 / 21.0),
    }
    q[5, 2] = z * q[2, 0]
    for m in range(DEGREES - 1):
        q[m + 1, m] = z
    cosine, sine = [w], [None]
    for m in range(1, DEGREES):
        if m == 1:
            cosine.append(w * x)
            sine.append(w * y)
        else:
            cosine.append(cosine[-1] * x - sine[-1] * y)
            sine.append(sine[-1] * x + cosine[-2] * y)
    out = []
    for l in range(DEGREES):
        for signed in range(-l, l + 1):
            m = abs(signed)
            trig = sine[m] if signed < 0 else cosine[m]
            out.append(trig if l == m else q[l, m] * trig)
    return out


def kernel(tiles, nblk, rows_dev, lists, place, own_m, one_m, two_m, own_v, one_v, two_v, harm, zeta, data, edges, tally, cols, ybuf, rbuf, acc, hbuf):
    span = tiles * nblk
    part = tiles * rows_dev
    base_meta = nblk * 4
    me = place[0]
    slab_parity = place[1]
    below = jnp.where(slab_parity == 0, 2, 1)
    above = 3 - below

    data[0:part, :] = own_v[...]
    data[part : 2 * part, :] = one_v[...]
    data[2 * part : 3 * part, :] = two_v[...]

    def seat(t):
        return jnp.bitwise_xor(t, me) if tiles == 2 else t

    for k in range(nblk):
        tally[k] = 0

    def add_edge(mine, array, t, blk):
        n = tally[mine]
        edges[mine, n] = array * part + seat(t) * rows_dev + blk * 4
        tally[mine] = n + 1

    def entry(meta, t, p):
        row = seat(t) * rows_dev + base_meta
        a = meta[row, 2 * p].astype(jnp.int32)
        b = meta[row, 2 * p + 1].astype(jnp.int32)
        h = b // span
        rem = b - h * span
        return a, h, rem // nblk, rem % nblk

    def length(meta, t):
        return meta[seat(t) * rows_dev + base_meta, 2 * lists].astype(jnp.int32)

    def own_list(p, c):
        a, h, t2, k2 = entry(own_m, me, p)
        add_edge(a, jnp.where(h == 0, 0, below), t2, k2)

        @pl.when((h == 0) & (t2 == me) & (k2 != a))
        def _():
            add_edge(k2, 0, me, a)

        return c

    lax.fori_loop(0, length(own_m, me), own_list, 0)

    def slab_list(meta, array, half, t):
        def body(p, c):
            a, h, t2, k2 = entry(meta, t, p)

            @pl.when((h == half) & (t2 == me))
            def _():
                add_edge(k2, array, t, a)

            return c

        lax.fori_loop(0, length(meta, t), body, 0)

    for t in range(tiles):

        @pl.when(t != me)
        def _():
            slab_list(own_m, 0, 0, t)

        @pl.when(slab_parity == 0)
        def _():
            slab_list(one_m, 1, 1, t)

        @pl.when(slab_parity == 1)
        def _():
            slab_list(two_m, 2, 1, t)

    scales = harmonic_scales()
    acc[...] = jnp.zeros_like(acc)
    for mine in range(nblk):
        home = mine * 4 + seat(me) * rows_dev

        def edge(e, c):
            row = edges[mine, e]
            px = data[pl.ds(home, 1), :]
            py = data[pl.ds(home + 1, 1), :]
            pz = data[pl.ds(home + 2, 1), :]
            other = jnp.concatenate([data[pl.ds(row + r, 1), :] for r in range(4)] * 2, axis=0)
            turned = other.T
            for r in range(4):
                cols[r] = jnp.broadcast_to(turned[:, r : r + 1], (128, 128))
            blk = (row % rows_dev) // 4
            dev_row = row - blk * 4 + base_meta

            def live_of(meta, off):
                return meta[dev_row - off, 2 * lists + 1 + blk].astype(jnp.int32)

            count = lax.cond(
                row < part,
                lambda: live_of(own_m, 0),
                lambda: lax.cond(row < 2 * part, lambda: live_of(one_m, part), lambda: live_of(two_m, 2 * part)),
            )

            def group(g, c2):
                for s in range(STEP):
                    at = pl.ds(pl.multiple_of((g * STEP + s) * SUB, SUB), SUB)
                    ex = cols[0, at, :] - px
                    ey = cols[1, at, :] - py
                    ez = cols[2, at, :] - pz
                    w = cols[3, at, :]
                    r2 = ex * ex + ey * ey + ez * ez
                    rs = lax.rsqrt(jnp.maximum(r2, 1e-30))
                    rho = r2 * rs
                    inv = jnp.minimum(rs, 1.0)
                    tau = rho * (1.0 / SPACING)
                    for b in range(NBIN):
                        rbuf[s, b] = jnp.maximum(0.0, 1.0 - jnp.abs(tau - (b + 1.0)))
                    for k, v in enumerate(harmonics_of(ex * inv, ey * inv, ez * inv, w)):
                        ybuf[s, k] = v
                for k in range(NHARM):
                    ys = [ybuf[s, k] for s in range(STEP)]
                    for b in range(NBIN):
                        t = ys[0] * rbuf[0, b]
                        for s in range(1, STEP):
                            t = t + ys[s] * rbuf[s, b]
                        acc[mine, k * BPAD + b] = acc[mine, k * BPAD + b] + t
                return c2

            lax.fori_loop(0, (count + STEP * SUB - 1) // (STEP * SUB), group, 0)
            return c

        lax.fori_loop(0, tally[mine], edge, 0)
        wlive = data[pl.ds(home + 3, 1), :]
        for k in range(NHARM):
            hk = jnp.sum(acc[mine, k * BPAD : (k + 1) * BPAD], axis=1) * scales[k]
            hbuf[k] = hk
            harm[mine, k * NBIN : (k + 1) * NBIN, :] = hk[:NBIN]
        for l in range(DEGREES):
            z = jnp.zeros((BPAD, BPAD), jnp.float32)
            for k in range(l * l, (l + 1) * (l + 1)):
                h = hbuf[k]
                z = z + lax.dot_general(h * wlive, h, (((1,), (1,)), ((), ())), precision=HIGH, preferred_element_type=jnp.float32)
            zeta[mine, l] = z * (1.0 / 128.0)


def shards(positions, weights, counts, pairs, pair_count):
    nblk, _, points = positions.shape
    lists = pairs.shape[1]
    tiles = lax.axis_size("tile")
    slabs = lax.axis_size("slab")
    slot = jnp.arange(points, dtype=jnp.int32)
    live = weights * (slot[None, :] < counts[:, None]).astype(jnp.float32)
    points_of = jnp.concatenate([positions, live[:, None, :]], axis=1).reshape(nblk * 4, points)
    meta = jnp.concatenate([pairs.reshape(-1), pair_count, counts]).astype(jnp.float32)
    rows_dev = -(-(nblk * 4 + 1) // 8) * 8
    packed = jnp.concatenate(
        [
            points_of,
            jnp.pad(meta, (0, points - meta.shape[0]))[None],
            jnp.zeros((rows_dev - nblk * 4 - 1, points), jnp.float32),
        ],
        axis=0,
    )
    both = ("slab", "tile")

    def move(value, hop):
        route = []
        for s in range(slabs):
            for t in range(tiles):
                s2, t2 = hop(s, t)
                if 0 <= s2 < slabs:
                    route.append((s * tiles + t, s2 * tiles + t2))
        return lax.ppermute(value, both, route)

    if tiles == 2:
        slab = jnp.concatenate([packed, move(packed, lambda s, t: (s, 1 - t))], axis=0)
    else:
        slab = lax.all_gather(packed, "tile", axis=0, tiled=True)
    near = move(slab, lambda s, t: (s + 1 - 2 * (s % 2), t))
    far = move(slab, lambda s, t: (s - 1 + 2 * (s % 2), t))
    place = jnp.stack([lax.axis_index("tile"), lax.axis_index("slab") % 2]).astype(jnp.int32)

    smem = pl.BlockSpec(memory_space=pltpu.SMEM)
    vmem = pl.BlockSpec(memory_space=pltpu.VMEM)
    body = lambda *refs: kernel(tiles, nblk, rows_dev, lists, *refs)
    harm, zeta = pl.pallas_call(
        body,
        out_shape=(
            jax.ShapeDtypeStruct((nblk, NHARM * NBIN, points), jnp.float32),
            jax.ShapeDtypeStruct((nblk, DEGREES, BPAD, BPAD), jnp.float32),
        ),
        in_specs=[smem] * 4 + [vmem] * 3,
        out_specs=(vmem, vmem),
        scratch_shapes=[
            pltpu.VMEM((3 * tiles * rows_dev, points), jnp.float32),
            pltpu.SMEM((nblk, lists * (2 * tiles + 1)), jnp.int32),
            pltpu.SMEM((nblk,), jnp.int32),
            pltpu.VMEM((4, points, points), jnp.float32),
            pltpu.VMEM((STEP, NHARM, SUB, points), jnp.float32),
            pltpu.VMEM((STEP, NBIN, SUB, points), jnp.float32),
            pltpu.VMEM((nblk, NHARM * BPAD, SUB, points), jnp.float32),
            pltpu.VMEM((NHARM, BPAD, points), jnp.float32),
        ],
    )(place, slab, near, far, slab, near, far)
    return harm, zeta[:, :, :NBIN, :NBIN].reshape(nblk, DEGREES, NBIN * NBIN)


def solution(mesh):
    return jax.shard_map(
        shards,
        mesh=mesh,
        in_specs=(
            P(("slab", "tile"), None, None),
            P(("slab", "tile"), None),
            P(("slab", "tile")),
            P(("slab", "tile"), None, None),
            P(("slab", "tile")),
        ),
        out_specs=(P(("slab", "tile"), None, None), P(("slab", "tile"), None, None)),
        check_vma=False,
    )
```

time: 312 us -> 40.5 us (0.13)
  the two profiles are of different devices: /device:TPU:1 before, /device:TPU:30 now
where the time goes in v1:
time: 40.5 us
  Pallas kernels  25.9 us (64%)
  waiting for transfers between devices  5.5 us (14%)
  local copies, waits for them, and re-layouts  3.62 us (9%)
  starting transfers between devices  2.59 us (6%)
  other arithmetic  1.52 us (4%)
  between operations  1.37 us (3%)
    pallas_call x1, Pallas kernels, shards(): pl.pallas_call(body, out_shape=(jax.ShapeDtypeStruct((nblk, NHARM * NBIN,...  25.9 us
    ppermute x3, waiting for transfers between devices, move(): return lax.ppermute(value, both, route)  5.5 us
    ppermute x3, starting transfers between devices, move(): return lax.ppermute(value, both, route)  2.59 us
    unnamed x13, local copies, waits for them, and re-layouts  1.94 us
    reshape x2, local copies, waits for them, and re-layouts, shards(): return (harm, zeta[:, :, :NBIN, :NBIN].reshape(nblk, DEGREES, NBIN * NBIN))  1.58 us
  transfers between devices with their start and end apart: 3, of which 2 were waited for; matrix products, arithmetic and copies ran while one was open for 2% of the time, Pallas kernels for 0%

profile of v1, /device:TPU:30, one launch (start us, length us, event | category | flops | bytes accessed | tf_op | source)
XLA Modules:
  0.0 40.5 jit_solution(7297661685754970384)
XLA Ops:
  0.6 0.0 copy-start.4
  0.6 0.0 copy-start.3
  1.3 0.0 copy-done.4
  1.3 0.7 %fusion = f32[2,1,128]{2,0,1:T(2,128)S(1)} fusion(f32[2,128]{1,0:T(2,128)} %param.6, s32[2]{0:T(128)S(1)} %copy-done.4), kind=kLoop, calls=%fused_computation.4 | loop fusion | flops 512 | bytes 2056 | tf_op jit(solution)/shard_map/broadcast_in_dim | solution.py:214
  2.1 0.0 copy-done.3
  2.1 0.0 copy-start.5
  2.1 0.7 %copy-done.5 = s32[1,8,2]{1,2,0:T(2,128)S(1)} copy-done((s32[1,8,2]{1,2,0:T(2,128)S(1)}, s32[1,8,2]{1,2,0:T(2,128)}, u32[]{:S(2)}) %copy-start.5) | copy-done | bytes 88
  2.8 0.1 copy.11
  2.8 0.1 reshape.15
  2.9 0.1 add_convert_fusion
  3.0 0.6 %collective-permute-start = (f32[16,128]{1,0:T(8,128)S(1)}, f32[16,128]{1,0:T(8,128)S(1)}, u32[]{:S(2)}, u32[]{:S(2)}) collective-permute-start(f32[16,128]{1,0:T(8,128)S(1)} %pad_maximum_fusion.1), channel_id=1, source_target_pairs={{0,1},{1,0},{2,3},{3,2},{4,5},{5,4},{6,7},{7,6},{8,9},{9,8},{10,11... | collective-permute-start | bytes 24584 | tf_op jit(solution)/shard_map/ppermute | solution.py:234
  3.6 3.1 %collective-permute-done = f32[16,128]{1,0:T(8,128)S(1)} collective-permute-done((f32[16,128]{1,0:T(8,128)S(1)}, f32[16,128]{1,0:T(8,128)S(1)}, u32[]{:S(2)}, u32[]{:S(2)}) %collective-permute-start) | collective-permute-done | bytes 8224 | tf_op jit(solution)/shard_map/ppermute | solution.py:234
  6.8 0.0 copy-start
  6.8 1.9 %collective-permute-start.2 = (f32[32,128]{1,0:T(8,128)S(1)}, f32[32,128]{1,0:T(8,128)S(1)}, u32[]{:S(2)}, u32[]{:S(2)}) collective-permute-start(f32[32,128]{1,0:T(8,128)S(1)} %pad_maximum_fusion.refs_1_.refs_4_), channel_id=1, source_target_pairs={{2,4},{3,5},{4,2},{5,3},{6,8},{7,9},{8,6},{9,7},{10,12},{11,13},{1... | collective-permute-start | bytes 49160 | tf_op jit(solution)/shard_map/ppermute | solution.py:234
  8.7 0.1 collective-permute-start.1
  8.8 0.7 %pad_add_fusion.refs_0_ = s32[2]{0:T(128)} fusion(s32[1]{0:T(128)} %bitcast.1, s32[1]{0:T(128)} %bitcast), kind=kLoop, calls=%fused_computation.5 | loop fusion | flops 2 | bytes 16 | tf_op jit(solution)/shard_map/stack | solution.py:242
  9.4 2.4 %collective-permute-done.2.refs_3_.refs_6_ = f32[32,128]{1,0:T(8,128)S(1)} collective-permute-done((f32[32,128]{1,0:T(8,128)S(1)}, f32[32,128]{1,0:T(8,128)S(1)}, u32[]{:S(2)}, u32[]{:S(2)}) %collective-permute-start.2) | collective-permute-done | bytes 16416 | tf_op jit(solution)/shard_map/ppermute | solution.py:234
  11.8 0.0 copy-start.1
  11.8 0.0 collective-permute-done.1.refs_2_.refs_5_
  11.8 0.0 copy-done
  11.8 0.6 %copy-done.1 = f32[32,128]{1,0:T(8,128)} copy-done((f32[32,128]{1,0:T(8,128)}, f32[32,128]{1,0:T(8,128)S(1)}, u32[]{:S(2)}) %copy-start.1) | copy-done | bytes 16408
  12.4 0.0 copy-start.2
  12.4 0.6 %copy-done.2 = f32[32,128]{1,0:T(8,128)} copy-done((f32[32,128]{1,0:T(8,128)}, f32[32,128]{1,0:T(8,128)S(1)}, u32[]{:S(2)}) %copy-start.2) | copy-done | bytes 16408
  13.0 25.9 %shard_map.68 = (f32[2,360,128]{2,1,0:T(8,128)}, f32[2,6,16,16]{3,2,1,0:T(8,128)}) custom-call(s32[2]{0:T(128)} %pad_add_fusion.refs_0_, f32[32,128]{1,0:T(8,128)} %copy-done, f32[32,128]{1,0:T(8,128)} %copy-done.2, f32[32,128]{1,0:T(8,128)} %copy-done.1, f32[32,128]{1,0:T(8,128)} %copy-done, f32[32,128]{1,0:T(8,128)} %copy-done.2, f32[32,128]{1,0:T(8,128)} %copy-done.1), custom_call_target="tpu_custom_call" | custom-call | tf_op jit(solution)/shard_map/pallas_call | solution.py:247
  38.9 1.0 %reshape.17 = f32[2,6,100]{2,1,0:T(8,128)S(1)} reshape(f32[2,6,10,10]{3,2,1,0:T(8,128)} %bitcast.8) | data formatting | bytes 9600 | tf_op jit(solution)/shard_map/reshape | solution.py:266
  39.9 0.6 %copy.13 = f32[2,6,100]{2,0,1:T(2,128)} copy(f32[2,6,100]{2,1,0:T(8,128)S(1)} %reshape.17) | data formatting | bytes 9600 | tf_op jit(solution)/shard_map/reshape | solution.py:266
  (6 shorter events, 0.0 us)
Async XLA Ops:
  0.6 0.7 %copy-start.4 = (s32[2]{0:T(128)S(1)}, s32[2]{0:T(128)}, u32[]{:S(2)}) copy-start(s32[2]{0:T(128)} %param.7) | copy-start | bytes 28
  0.6 1.4 %copy-start.3 = (f32[2,3,128]{2,0,1:T(2,128)S(1)}, f32[2,3,128]{2,0,1:T(2,128)}, u32[]{:S(2)}) copy-start(f32[2,3,128]{2,0,1:T(2,128)} %param.5) | copy-start | bytes 9220
  2.1 0.7 %copy-start.5 = (s32[1,8,2]{1,2,0:T(2,128)S(1)}, s32[1,8,2]{1,2,0:T(2,128)}, u32[]{:S(2)}) copy-start(s32[1,8,2]{1,2,0:T(2,128)} %param.8) | copy-start | bytes 196
  3.0 3.7 %collective-permute-start = (f32[16,128]{1,0:T(8,128)S(1)}, f32[16,128]{1,0:T(8,128)S(1)}, u32[]{:S(2)}, u32[]{:S(2)}) collective-permute-start(f32[16,128]{1,0:T(8,128)S(1)} %pad_maximum_fusion.1), channel_id=1, source_target_pairs={{0,1},{1,0},{2,3},{3,2},{4,5},{5,4},{6,7},{7,6},{8,9},{9,8},{10,11... | collective-permute-start | bytes 24584 | tf_op jit(solution)/shard_map/ppermute | solution.py:234
  6.8 5.1 %copy-start = (f32[32,128]{1,0:T(8,128)}, f32[32,128]{1,0:T(8,128)S(1)}, u32[]{:S(2)}) copy-start(f32[32,128]{1,0:T(8,128)S(1)} %pad_maximum_fusion.refs_1_.refs_4_) | copy-start | bytes 49156
  6.8 5.1 %collective-permute-start.2 = (f32[32,128]{1,0:T(8,128)S(1)}, f32[32,128]{1,0:T(8,128)S(1)}, u32[]{:S(2)}, u32[]{:S(2)}) collective-permute-start(f32[32,128]{1,0:T(8,128)S(1)} %pad_maximum_fusion.refs_1_.refs_4_), channel_id=1, source_target_pairs={{2,4},{3,5},{4,2},{5,3},{6,8},{7,9},{8,6},{9,7},{10,12},{11,13},{1... | collective-permute-start | bytes 49160 | tf_op jit(solution)/shard_map/ppermute | solution.py:234
  8.7 3.1 %collective-permute-start.1 = (f32[32,128]{1,0:T(8,128)S(1)}, f32[32,128]{1,0:T(8,128)S(1)}, u32[]{:S(2)}, u32[]{:S(2)}) collective-permute-start(f32[32,128]{1,0:T(8,128)S(1)} %pad_maximum_fusion.refs_1_.refs_4_), channel_id=1, source_target_pairs={{0,2},{1,3},{2,0},{3,1},{4,6},{5,7},{6,4},{7,5},{8,10},{9,11},{10,... | collective-permute-start | bytes 49160 | tf_op jit(solution)/shard_map/ppermute | solution.py:234
  11.8 0.6 %copy-start.1 = (f32[32,128]{1,0:T(8,128)}, f32[32,128]{1,0:T(8,128)S(1)}, u32[]{:S(2)}) copy-start(f32[32,128]{1,0:T(8,128)S(1)} %collective-permute-done.2.refs_3_.refs_6_) | copy-start | bytes 49156
  12.4 0.6 %copy-start.2 = (f32[32,128]{1,0:T(8,128)}, f32[32,128]{1,0:T(8,128)S(1)}, u32[]{:S(2)}) copy-start(f32[32,128]{1,0:T(8,128)S(1)} %collective-permute-done.1.refs_2_.refs_5_) | copy-start | bytes 49156
